TPU v7x, 128 devices: a whole 4x4x4 slice. The times are simulated.
128 devices in a mesh: rep: 16 (over x_lo, y, core), fsdp: 8 (over x_hi, z).
Axes of the slice: x: 4 (x_hi: 2, x_lo: 2; x = x_hi * 2 + x_lo), y: 4, z: 4, core: 2. Of those that a mesh axis runs over, the one named last changes fastest.
Arguments:
- tokens: bfloat16 [131072, 8192], P(('rep', 'fsdp')), may hold values from -6 to 6
- norm_gain: bfloat16 [8192], replicated, may hold values from 0.25 to 1.75
- deltas: bfloat16 [16, 8192, 1024], P('rep', 'fsdp'), may hold values from -0.09375 to 0.09375
- inner_steps: int32 [16, 16], replicated, may hold values from 1 to 64
- bucket_of_row: int32 [8192], P('fsdp'), may hold values from 0 to 15, never falling along the last dimension, each value on 1 to 1024 neighbouring positions
- master: float32 [8192, 1024], P(('fsdp', 'rep')), may hold values from -0.0625 to 0.0625
- momentum: float32 [8192, 1024], P(('fsdp', 'rep')), may hold values from -0.0625 to 0.0625
Outputs:
- keys: bfloat16 [131072, 1024], P(('rep', 'fsdp'))
- master_new: float32 [8192, 1024], P(('fsdp', 'rep'))
- momentum_new: float32 [8192, 1024], P(('fsdp', 'rep'))
Inputs may be any that keep to these rules, and one draw needn't show every extreme that they name: `bucket_of_row`: never falls along the rows; each bucket holds 1 to 1024 rows.
All inputs are finite; a program needn't handle non-finite values.
Results may differ from a plain program's by a relative error of at most 0.0058.
Values may be sent and summed in bfloat16 or wider, within the bound.
A program may use at most 192 MiB of HBM per device.

v0:
```python
import jax
import jax.numpy as jnp
from jax import lax
from jax.sharding import PartitionSpec as P

OUTER_RATE = 0.7
MOMENTUM_KEEP = 0.9
EPSILON = 1e-05


def normalize(rows, norm_gain):
    values = rows.astype(jnp.float32)
    scale = lax.rsqrt(jnp.mean(values * values, axis=1, keepdims=True) + EPSILON)
    return (values * scale * norm_gain.astype(jnp.float32)[None, :]).astype(jnp.bfloat16)


def on_device(tokens, norm_gain, deltas, inner_steps, bucket_of_row, master, momentum):
    counts = inner_steps.astype(jnp.float32)
    share = counts / jnp.sum(counts, axis=0, keepdims=True)
    own_share = lax.dynamic_slice_in_dim(share, lax.axis_index("rep"), 1, 0)[0]
    bucket_ids = jnp.arange(counts.shape[1], dtype=jnp.int32)
    one_hot = (bucket_of_row[:, None] == bucket_ids[None, :]).astype(jnp.float32)
    row_weight = jnp.sum(one_hot * own_share[None, :], axis=1)
    weighted = row_weight[:, None] * deltas[0].astype(jnp.float32)
    averaged = lax.psum_scatter(weighted, "rep", scatter_dimension=0, tiled=True)
    momentum_new = MOMENTUM_KEEP * momentum + averaged
    master_new = master - OUTER_RATE * (averaged + MOMENTUM_KEEP * momentum_new)
    layer = master_new.astype(jnp.bfloat16)
    normed = normalize(tokens, norm_gain)
    fsdp_count = lax.axis_size("fsdp")
    rep_count = lax.axis_size("rep")
    shard_len = layer.shape[0]
    piece = lax.all_gather(layer, ("rep", "fsdp"), axis=0, tiled=True)
    order = jnp.arange(piece.shape[0], dtype=jnp.int32)
    shard = order // shard_len
    within = order % shard_len
    rep_pos = shard // fsdp_count
    fsdp_pos = shard % fsdp_count
    column_ids = (fsdp_pos * rep_count + rep_pos) * shard_len + within
    columns = jnp.take(normed, column_ids, axis=1)
    projected = jnp.dot(columns, piece, preferred_element_type=jnp.float32)
    return (projected.astype(jnp.bfloat16), master_new, momentum_new)


def solution(mesh):
    in_specs = (
        P(("rep", "fsdp"), None),
        P(),
        P("rep", "fsdp", None),
        P(),
        P("fsdp"),
        P(("fsdp", "rep"), None),
        P(("fsdp", "rep"), None),
    )
    out_specs = (P(("rep", "fsdp"), None), P(("fsdp", "rep"), None), P(("fsdp", "rep"), None))
    return jax.shard_map(
        on_device, mesh=mesh, in_specs=in_specs, out_specs=out_specs, check_vma=False
    )
```

profile of v0, /device:TPU:1, one launch (start us, length us, event | category | flops | bytes accessed | tf_op | source)
XLA Modules:
  0.0 442.1 jit_solution(9010786290908330354)
XLA Ops:
  7.2 0.0 reduce-scatter.2.cloned.1.call-start
  7.2 0.7 convert_element_type.28
  7.9 0.7 convert_reduce_fusion
  8.6 0.8 select_reduce_fusion
  9.4 3.9 convert_multiply_fusion.2
  13.3 0.0 reduce-scatter.2.cloned.1.call-update
  13.3 0.0 all-gather.2.cloned.1.call-start
  13.3 66.3 %reduce-scatter.2.cloned.1.call-done = f32[64,1024]{1,0:T(8,128)} async-done(((f32[1024,1024]{1,0:T(8,128)}), f32[64,1024]{1,0:T(8,128)}) %reduce-scatter.2.cloned.1.call-update) | async-done | bytes 262160 | tf_op jit(solution)/shard_map/reduce_scatter | solution.py:25
  79.7 2.0 fusion.33
  81.7 0.0 all-gather.2.cloned.1.call-update
  81.7 0.0 copy-start.1
  81.7 22.4 %copy.12 = bf16[1024,8192]{0,1:T(8,128)(2,1)} copy(bf16[1024,8192]{1,0:T(8,128)(2,1)} %param.7) | data formatting | bytes 33554432 | tf_op args[0]
  104.2 0.0 copy-done.1
  104.2 0.0 copy-start
  104.2 10.5 %fusion = f32[1024]{0:T(1024)S(1)} fusion(bf16[1024,8192]{0,1:T(8,128)(2,1)} %copy.12), kind=kLoop, calls=%fused_computation.3 | loop fusion | flops 25164800 | bytes 16781312 | tf_op jit(solution)/shard_map/reduce_sum | solution.py:13
  114.7 0.1 compare_select_fusion
  114.8 0.5 copy-done
  115.3 8.0 %fusion.2 = bf16[1024,8192]{0,1:T(8,128)(2,1)} fusion(bf16[1024,8192]{0,1:T(8,128)(2,1)S(1)} %copy-done, f32[8192]{0:T(1024)S(1)} %convert_element_type.26, f32[1024]{0:T(1024)S(1)} %add_rsqrt_fusion), kind=kLoop, calls=%fused_computation.5 | loop fusion | flops 33554432 | bytes 33591296 | tf_op jit(solution)/shard_map/convert_element_type | solution.py:14
  123.3 48.7 %gather_fusion = bf16[8192,1024]{1,0:T(8,128)(2,1)} fusion(bf16[1024,8192]{0,1:T(8,128)(2,1)} %fusion.2, s32[8192]{0:T(1024)S(1)} %broadcast_clamp_fusion), kind=kCustom, calls=%fused_computation | custom fusion | bytes 33587200 | tf_op jit(solution)/shard_map/jit(_take)/gather | solution.py:40
  172.0 239.4 %all-gather.2.cloned.1.call-done = bf16[8192,1024]{1,0:T(8,128)(2,1)} async-done(((bf16[64,1024]{1,0:T(8,128)(2,1)}), bf16[8192,1024]{1,0:T(8,128)(2,1)}) %all-gather.2.cloned.1.call-update) | async-done | bytes 16777232 | tf_op jit(solution)/shard_map/all_gather | solution.py:33
  411.4 23.8 %fusion.7 = bf16[1024,1024]{1,0:T(8,128)(2,1)} fusion(bf16[8192,1024]{1,0:T(8,128)(2,1)} %all-gather.2.cloned.1.call-done, bf16[8192,1024]{1,0:T(8,128)(2,1)} %gather_fusion, pred[8192]{0:T(1024)(128)(4,1)S(1)} %compare_and_fusion), kind=kOutput, calls=%fused_computation.11 | convolution fusion | flops 17189306368 | bytes 35659776 | tf_op jit(solution)/shard_map/dot_general | solution.py:41
  (5 shorter events, 0.1 us)
Async XLA Ops:
  7.2 72.5 %reduce-scatter.2.cloned.1.call-start = ((), (), s32[]{:S(2)}) async-start(), calls=%async_computation.1 | async-start | bytes 4456448 | tf_op jit(solution)/shard_map/reduce_scatter | solution.py:25
  13.3 398.1 %all-gather.2.cloned.1.call-start = ((), (), s32[]{:S(2)}) async-start(), calls=%async_computation.2 | async-start | bytes 16908288 | tf_op jit(solution)/shard_map/all_gather | solution.py:33
  81.7 22.4 %copy-start.1 = (bf16[8192]{0:T(1024)(128)(2,1)S(1)}, bf16[8192]{0:T(1024)(128)(2,1)}, u32[]{:S(2)}) copy-start(bf16[8192]{0:T(1024)(128)(2,1)} %param.8) | copy-start | bytes 49156
  104.2 11.1 %copy-start = (bf16[1024,8192]{0,1:T(8,128)(2,1)S(1)}, bf16[1024,8192]{0,1:T(8,128)(2,1)}, u32[]{:S(2)}) copy-start(bf16[1024,8192]{0,1:T(8,128)(2,1)} %copy.12) | copy-start | bytes 50331652
Sparse Core Ops, SparseCore 0:
  13.4 66.2 reduce-scatter.1
  81.9 329.4 all-gather.1
where the time goes:
time: 443 us; the launch traced here: 442 us
  waiting for transfers between devices  306 us (69%)
  local copies, waits for them, and re-layouts  71.6 us (16%)
  other arithmetic  26.7 us (6%)
  matrix products  23.8 us (5%)
  between operations  14.1 us (3%)
    all_gather x1, waiting for transfers between devices, on_device(): piece = lax.all_gather(layer, ('rep', 'fsdp'), axis=0, tiled=True)  239 us
    reduce_scatter x1, waiting for transfers between devices, on_device(): lax.psum_scatter(weighted, 'rep', scatter_dimension=0, tiled=True)  66.3 us
    gather x1, local copies, waits for them, and re-layouts, on_device(): columns = jnp.take(normed, column_ids, axis=1)  48.7 us
    dot_general x1, matrix products, on_device(): projected = jnp.dot(columns, piece, preferred_element_type=jnp.float32)  23.8 us
    unnamed x5, local copies, waits for them, and re-layouts  22.9 us
    reduce_sum x1, other arithmetic, normalize(): jnp.mean(values * values, axis=1, keepdims=True) + EPSILON  10.5 us
  transfers between devices with their start and end apart: 2, of which 2 were waited for; matrix products, arithmetic and copies ran while one was open for 20% of the time, Pallas kernels for 0%

commit v1 on v0

--- a/solution.py
+++ b/solution.py
@@ -30,7 +30,10 @@
     fsdp_count = lax.axis_size("fsdp")
     rep_count = lax.axis_size("rep")
     shard_len = layer.shape[0]
-    piece = lax.all_gather(layer, ("rep", "fsdp"), axis=0, tiled=True)
+    piece = jnp.concatenate(
+        lax.all_to_all(jnp.stack([layer] * lax.axis_size(("rep", "fsdp"))), ("rep", "fsdp"), 0, 0),
+        axis=0,
+    )
     order = jnp.arange(piece.shape[0], dtype=jnp.int32)
     shard = order // shard_len
     within = order % shard_len

time: 443 us -> 368 us (0.83)
  waiting for transfers between devices: 306 us -> 215 us
  starting transfers between devices: 0.08 us -> 11 us
  local copies, waits for them, and re-layouts: 71.6 us -> 77.3 us
    all_gather x1 -> x0, waiting for transfers between devices: 239 us -> none  [on_device(): piece = lax.all_gather(layer, ('rep', 'fsdp'), axis=0, tiled=True)]
    all_to_all x0 -> x1, waiting for transfers between devices: none -> 148 us  [on_device(): lax.all_to_all(jnp.stack([layer] * lax.axis_size(('rep', 'fsdp'))), ('rep...]
    all_to_all x0 -> x1, starting transfers between devices: none -> 11 us  [on_device(): lax.all_to_all(jnp.stack([layer] * lax.axis_size(('rep', 'fsdp'))), ('rep...]
    another operation x0 -> x1, local copies, waits for them, and re-layouts: none -> 5.99 us  [on_device(): jnp.stack([layer] * lax.axis_size(('rep', 'fsdp')))]
  transfers between devices with their start and end apart: 2 -> 2, of which waited for: 2 -> 2; matrix products, arithmetic and copies ran while one was open for 20% -> 24% of each run, Pallas kernels for 0% -> 0%
where the time goes in v1:
time: 368 us
  waiting for transfers between devices  215 us (58%)
  local copies, waits for them, and re-layouts  77.3 us (21%)
  other arithmetic  26.6 us (7%)
  matrix products  23.8 us (6%)
  between operations  14.1 us (4%)
  starting transfers between devices  11 us (3%)
    all_to_all x1, waiting for transfers between devices, on_device(): lax.all_to_all(jnp.stack([layer] * lax.axis_size(('rep', 'fsdp'))), ('rep...  148 us
    reduce_scatter x1, waiting for transfers between devices, on_device(): lax.psum_scatter(weighted, 'rep', scatter_dimension=0, tiled=True)  66.4 us
    gather x1, local copies, waits for them, and re-layouts, on_device(): columns = jnp.take(normed, column_ids, axis=1)  48.5 us
    dot_general x1, matrix products, on_device(): projected = jnp.dot(columns, piece, preferred_element_type=jnp.float32)  23.8 us
    unnamed x5, local copies, waits for them, and re-layouts  22.7 us
    all_to_all x1, starting transfers between devices, on_device(): lax.all_to_all(jnp.stack([layer] * lax.axis_size(('rep', 'fsdp'))), ('rep...  11 us
    reduce_sum x1, other arithmetic, normalize(): jnp.mean(values * values, axis=1, keepdims=True) + EPSILON  10.5 us
    convert_element_type x1, other arithmetic, normalize(): (values * scale * norm_gain.astype(jnp.float32)[None, :]).astype(jnp.bflo...  7.98 us
  transfers between devices with their start and end apart: 2, of which 2 were waited for; matrix products, arithmetic and copies ran while one was open for 24% of the time, Pallas kernels for 0%

profile of v1, /device:TPU:1, one launch (start us, length us, event | category | flops | bytes accessed | tf_op | source)
XLA Modules:
  0.0 367.6 jit_solution(9912960587243006318)
XLA Ops:
  7.2 0.0 reduce-scatter.2.cloned.1.call-start
  7.2 0.7 convert_element_type.28
  7.9 0.7 convert_reduce_fusion
  8.6 0.8 select_reduce_fusion
  9.4 3.9 %convert_multiply_fusion.2 = f32[1024,1024]{1,0:T(8,128)} fusion(bf16[1,1024,1024]{2,1,0:T(8,128)(2,1)} %param.9, f32[1024]{0:T(1024)S(1)} %select_reduce_fusion), kind=kLoop, calls=%fused_computation.10 | loop fusion | flops 2097152 | bytes 6295552 | tf_op jit(solution)/shard_map/mul | solution.py:24
  13.3 0.0 reduce-scatter.2.cloned.1.call-update
  13.3 66.4 %reduce-scatter.2.cloned.1.call-done = f32[64,1024]{1,0:T(8,128)} async-done(((f32[1024,1024]{1,0:T(8,128)}), f32[64,1024]{1,0:T(8,128)}) %reduce-scatter.2.cloned.1.call-update) | async-done | bytes 262160 | tf_op jit(solution)/shard_map/reduce_scatter | solution.py:25
  79.7 2.0 fusion.33
  81.6 6.0 %stack.2 = bf16[128,64,1024]{2,1,0:T(8,128)(2,1)} broadcast(bf16[64,1024]{1,0:T(8,128)(2,1)S(1)} %get-tuple-element.3), dimensions={1,2} | broadcast | bytes 16908288 | tf_op jit(solution)/shard_map/stack | solution.py:34
  87.6 11.0 %all-to-all-start = ((bf16[128,64,1024]{2,1,0:T(8,128)(2,1)}), bf16[128,64,1024]{2,1,0:T(8,128)(2,1)}, u32[]{:S(2)}, u32[]{:S(2)}) async-start(bf16[128,64,1024]{2,1,0:T(8,128)(2,1)} %stack.2), calls=%async_computation.1 | async-start | bytes 33554432 | tf_op jit(solution)/shard_map/all_to_all | solution.py:34
  98.6 0.0 copy-start.1
  98.6 22.4 %copy.12 = bf16[1024,8192]{0,1:T(8,128)(2,1)} copy(bf16[1024,8192]{1,0:T(8,128)(2,1)} %param.7) | data formatting | bytes 33554432 | tf_op args[0]
  121.1 0.0 copy-done.1
  121.1 0.0 copy-start
  121.1 10.5 %fusion = f32[1024]{0:T(1024)S(1)} fusion(bf16[1024,8192]{0,1:T(8,128)(2,1)} %copy.12), kind=kLoop, calls=%fused_computation.3 | loop fusion | flops 25164800 | bytes 16781312 | tf_op jit(solution)/shard_map/reduce_sum | solution.py:13
  131.6 0.1 compare_select_fusion
  131.7 0.3 copy-done
  132.0 8.0 %fusion.2 = bf16[1024,8192]{0,1:T(8,128)(2,1)} fusion(bf16[1024,8192]{0,1:T(8,128)(2,1)S(1)} %copy-done, f32[8192]{0:T(1024)S(1)} %convert_element_type.26, f32[1024]{0:T(1024)S(1)} %add_rsqrt_fusion), kind=kLoop, calls=%fused_computation.5 | loop fusion | flops 33554432 | bytes 33591296 | tf_op jit(solution)/shard_map/convert_element_type | solution.py:14
  140.0 48.5 %gather_fusion = bf16[8192,1024]{1,0:T(8,128)(2,1)} fusion(bf16[1024,8192]{0,1:T(8,128)(2,1)} %fusion.2, s32[8192]{0:T(1024)S(1)} %broadcast_clamp_fusion), kind=kCustom, calls=%fused_computation | custom fusion | bytes 33587200 | tf_op jit(solution)/shard_map/jit(_take)/gather | solution.py:43
  188.5 148.4 %all-to-all-done = bf16[128,64,1024]{2,1,0:T(8,128)(2,1)} async-done(((bf16[128,64,1024]{2,1,0:T(8,128)(2,1)}), bf16[128,64,1024]{2,1,0:T(8,128)(2,1)}, u32[]{:S(2)}, u32[]{:S(2)}) %all-to-all-start) | async-done | bytes 16777248 | tf_op jit(solution)/shard_map/all_to_all | solution.py:34
  336.9 23.8 %fusion.7 = bf16[1024,1024]{1,0:T(8,128)(2,1)} fusion(bf16[8192,1024]{1,0:T(8,128)(2,1)} %bitcast.3, bf16[8192,1024]{1,0:T(8,128)(2,1)} %gather_fusion, pred[8192]{0:T(1024)(128)(4,1)S(1)} %compare_and_fusion), kind=kOutput, calls=%fused_computation.11 | convolution fusion | flops 17189306368 | bytes 35659776 | tf_op jit(solution)/shard_map/dot_general | solution.py:44
  (5 shorter events, 0.1 us)
Async XLA Ops:
  7.2 72.5 %reduce-scatter.2.cloned.1.call-start = ((), (), s32[]{:S(2)}) async-start(), calls=%async_computation.2 | async-start | bytes 4456448 | tf_op jit(solution)/shard_map/reduce_scatter | solution.py:25
  87.6 249.3 %all-to-all-start = ((bf16[128,64,1024]{2,1,0:T(8,128)(2,1)}), bf16[128,64,1024]{2,1,0:T(8,128)(2,1)}, u32[]{:S(2)}, u32[]{:S(2)}) async-start(bf16[128,64,1024]{2,1,0:T(8,128)(2,1)} %stack.2), calls=%async_computation.1 | async-start | bytes 33554432 | tf_op jit(solution)/shard_map/all_to_all | solution.py:34
  98.6 22.5 %copy-start.1 = (bf16[8192]{0:T(1024)(128)(2,1)S(1)}, bf16[8192]{0:T(1024)(128)(2,1)}, u32[]{:S(2)}) copy-start(bf16[8192]{0:T(1024)(128)(2,1)} %param.8) | copy-start | bytes 49156
  121.1 10.9 %copy-start = (bf16[1024,8192]{0,1:T(8,128)(2,1)S(1)}, bf16[1024,8192]{0,1:T(8,128)(2,1)}, u32[]{:S(2)}) copy-start(bf16[1024,8192]{0,1:T(8,128)(2,1)} %copy.12) | copy-start | bytes 50331652
Sparse Core Ops, SparseCore 0:
  13.4 66.2 reduce-scatter.1
